TPU v7x, 32 devices: a whole 2x2x4 slice. The times are simulated.
32 devices in a mesh: blk: 8 (over y, x, core), slab: 4 (over z).
Axes of the slice: x: 2, y: 2, z: 4, core: 2. Of those that a mesh axis runs over, the one named last changes fastest.
Arguments:
- old_factor: bfloat16 [8192, 24576], P('slab', 'blk'), may hold values from -0.0546875 to 0.0546875
- solved: bfloat16 [24576, 256], P('blk', 'slab'), may hold values from -6 to 6
- band: bfloat16 [8192, 8192], P('blk'), may hold values from -0.0625 to 0.0625
- inv_diag: bfloat16 [2048, 8192], P(None, 'blk'), may hold values from -1 to 2, as said below
- rhs: bfloat16 [8192, 256], P('blk', 'slab'), may hold values from -6 to 6
Outputs:
- solution: bfloat16 [8192, 256], P('blk', 'slab')
Inputs may be any that keep to these rules, and one draw needn't show every extreme that they name: `inv_diag`: columns k * 2048 to (k + 1) * 2048 - 1 hold the inverse applied in block step k.
All inputs are finite; a program needn't handle non-finite values.
Results may differ from a plain program's by a relative error of at most 0.008.
Values may be sent and summed in bfloat16 or wider, within the bound.
A program may use at most 64 MiB of HBM per device.

v0:
```python
import jax
import jax.numpy as jnp
from jax import lax
from jax.sharding import PartitionSpec as P

STEPS = 4


def body(old_factor, solved, band, inv_diag, rhs):
    own_rows = rhs.shape[0]
    block_rows = inv_diag.shape[0]
    group_size = block_rows // own_rows
    own_index = lax.axis_index("blk")
    own_block = own_index // group_size
    offset = own_index % group_size * own_rows
    partial_value = jnp.dot(
        old_factor,
        lax.all_gather(solved, "slab", axis=1, tiled=True),
        preferred_element_type=jnp.float32,
    )
    window_terms = lax.all_to_all(partial_value, "slab", split_axis=1, concat_axis=0, tiled=True)
    source = rhs.astype(jnp.float32)
    accum = lax.psum_scatter(window_terms, "blk", scatter_dimension=0, tiled=True)
    solution = jnp.zeros(rhs.shape, jnp.bfloat16)
    for step in range(STEPS):
        total = accum
        resid = (source - total).astype(jnp.bfloat16)
        term = jnp.dot(inv_diag, resid, preferred_element_type=jnp.float32)
        term = jnp.where(own_block == step, term, jnp.zeros_like(term))
        newest = lax.psum(term, "blk").astype(jnp.bfloat16)
        mine = lax.dynamic_slice_in_dim(newest, offset, own_rows, 0)
        solution = jnp.where(own_block == step, mine, solution)
        if step + 1 < STEPS:
            columns = band[:, step * block_rows : (step + 1) * block_rows]
            update = jnp.dot(columns, newest, preferred_element_type=jnp.float32)
            accum = accum + jnp.where(own_block > step, update, jnp.zeros_like(update))
    return solution


def solution(mesh):
    return jax.shard_map(
        body,
        mesh=mesh,
        in_specs=(
            P("slab", "blk"),
            P("blk", "slab"),
            P("blk", None),
            P(None, "blk"),
            P("blk", "slab"),
        ),
        out_specs=P("blk", "slab"),
        check_vma=False,
    )
```

profile of v0, /device:TPU:0, one launch (start us, length us, event | category | flops | bytes accessed | tf_op | source)
XLA Modules:
  0.0 292.5 jit_solution(17000383142873836997)
XLA Ops:
  6.5 0.0 all-gather.2.cloned.1.call-start
  6.5 0.7 all-gather.2.cloned.1.call-update
  7.3 0.0 reduce-scatter.2.cloned.1.call-start
  7.3 41.4 %all-gather.2.cloned.1.call-done = bf16[3072,256]{0,1:T(8,128)(2,1)} async-done(((bf16[3072,64]{0,1:T(8,128)(2,1)}), bf16[3072,256]{0,1:T(8,128)(2,1)}) %all-gather.2.cloned.1.call-update) | async-done | bytes 1572880 | tf_op jit(solution)/shard_map/all_gather | solution.py:18
  48.7 6.9 %fusion.56 = f32[2048,256]{0,1:T(8,128)S(1)} fusion(bf16[2048,3072]{1,0:T(8,128)(2,1)} %param.5, bf16[3072,256]{0,1:T(8,128)(2,1)} %all-gather.2.cloned.1.call-done), kind=kOutput, calls=%fused_computation.37 | convolution fusion | flops 3221225472 | bytes 16252928 | tf_op jit(solution)/shard_map/dot_general | solution.py:16
  55.6 50.4 %all_to_all.19 = f32[2048,4,64]{0,2,1:T(8,128)S(1)} all-to-all(f32[2048,4,64]{0,2,1:T(8,128)S(1)} %bitcast.41), channel_id=1, replica_groups=mesh['blk'=8,'slab'=4] {'slab'}, dimensions={1} | all-to-all | bytes 4194304 | tf_op jit(solution)/shard_map/all_to_all | solution.py:21
  106.0 0.0 copy-start.2
  106.0 1.5 copy.7
  107.5 0.0 reduce-scatter.2.cloned.1.call-update
  107.6 40.6 %reduce-scatter.2.cloned.1.call-done = f32[1024,64]{0,1:T(8,128)} async-done(((f32[8192,64]{0,1:T(8,128)}), f32[1024,64]{0,1:T(8,128)}) %reduce-scatter.2.cloned.1.call-update) | async-done | bytes 262160 | tf_op jit(solution)/shard_map/reduce_scatter | solution.py:23
  148.2 0.0 copy-done.2
  148.2 0.0 copy-start.3
  148.2 3.7 %fusion.6 = f32[2048,64]{0,1:T(8,128)S(1)} fusion(bf16[2048,1024]{1,0:T(8,128)(2,1)} %param.8, pred[]{:T(512)S(6)} %eq.19, f32[1024,64]{0,1:T(8,128)} %reduce-scatter.2.cloned.1.call-done, bf16[1024,64]{0,1:T(8,128)(2,1)S(1)} %copy-done.2), kind=kOutput, calls=%fused_computation.10 | convolution fusion | flops 268763136 | bytes 5111809 | tf_op jit(solution)/shard_map/dot_general | solution.py:28
  151.9 29.6 %all-reduce.4 = bf16[2048,64]{0,1:T(8,128)(2,1)S(1)} all-reduce(f32[2048,64]{0,1:T(8,128)S(1)} %fusion.6), channel_id=1, replica_groups=mesh['blk'=8,'slab'=4] {'blk'}, use_global_device_ids=true, to_apply=%region_1.2 | all-reduce | flops 131072 | bytes 786432 | tf_op jit(solution)/shard_map/psum | solution.py:30
  181.5 0.0 copy-done.3
  181.5 0.0 copy-start
  181.5 3.7 %fusion.16 = f32[1024,64]{0,1:T(8,128)S(1)} fusion(f32[1024,64]{0,1:T(8,128)S(1)} %copy-done.3, bf16[2048,64]{0,1:T(8,128)(2,1)S(1)} %all-reduce.4, bf16[1024,8192]{1,0:T(8,128)(2,1)} %param.7, pred[]{:T(512)S(6)} %gt.9), kind=kOutput, calls=%fused_computation.16 | convolution fusion | flops 268566528 | bytes 4980737 | tf_op jit(solution)/shard_map/dot_general | solution.py:35
  185.3 0.0 copy-done
  185.3 1.4 fusion.7
  186.7 29.4 %all-reduce.5 = bf16[2048,64]{0,1:T(8,128)(2,1)S(1)} all-reduce(f32[2048,64]{0,1:T(8,128)S(1)} %fusion.7), channel_id=1, replica_groups=mesh['blk'=8,'slab'=4] {'blk'}, use_global_device_ids=true, to_apply=%region_2.3 | all-reduce | flops 131072 | bytes 786432 | tf_op jit(solution)/shard_map/psum | solution.py:30
  216.1 0.0 copy-start.1
  216.1 3.7 %fusion.25 = f32[1024,64]{0,1:T(8,128)S(1)} fusion(f32[1024,64]{0,1:T(8,128)S(1)} %fusion.16, bf16[2048,64]{0,1:T(8,128)(2,1)S(1)} %all-reduce.5, bf16[1024,8192]{1,0:T(8,128)(2,1)} %param.7, pred[]{:T(512)S(6)} %gt.10), kind=kOutput, calls=%fused_computation.19 | convolution fusion | flops 268566528 | bytes 4980737 | tf_op jit(solution)/shard_map/dot_general | solution.py:35
  219.8 0.0 copy-done.1
  219.8 1.4 fusion.8
  221.2 28.8 %all-reduce.6 = bf16[2048,64]{0,1:T(8,128)(2,1)S(1)} all-reduce(f32[2048,64]{0,1:T(8,128)S(1)} %fusion.8), channel_id=1, replica_groups=mesh['blk'=8,'slab'=4] {'blk'}, use_global_device_ids=true, to_apply=%region_3.4 | all-reduce | flops 131072 | bytes 786432 | tf_op jit(solution)/shard_map/psum | solution.py:30
  250.0 6.2 %fusion.9 = f32[2048,64]{0,1:T(8,128)S(1)} fusion(bf16[2048,1024]{1,0:T(8,128)(2,1)} %param.8, f32[1024,64]{0,1:T(8,128)S(1)} %fusion.25, bf16[2048,64]{0,1:T(8,128)(2,1)S(1)} %all-reduce.6, bf16[1024,8192]{1,0:T(8,128)(2,1)} %param.7, bf16[1024,64]{0,1:T(8,128)(2,1)S(1)} %copy-done.2, pred[]{:T(512)S(6)} %eq.18, pred[]{:T(512)S(6)} %gt.11), kind=kOutput, calls=%fused_computation.13 | convolution fusion | flops 537329664 | bytes 9568258 | tf_op jit(solution)/shard_map/dot_general | solution.py:28
  256.2 28.8 %all-reduce.7 = bf16[2048,64]{0,1:T(8,128)(2,1)S(1)} all-reduce(f32[2048,64]{0,1:T(8,128)S(1)} %fusion.9), channel_id=1, replica_groups=mesh['blk'=8,'slab'=4] {'blk'}, use_global_device_ids=true, to_apply=%region_4.5 | all-reduce | flops 131072 | bytes 786432 | tf_op jit(solution)/shard_map/psum | solution.py:30
  284.9 0.7 fusion.49
Async XLA Ops:
  6.5 42.1 %all-gather.2.cloned.1.call-start = ((), (), s32[]{:S(2)}) async-start(), calls=%async_computation.2 | async-start | bytes 1966080 | tf_op jit(solution)/shard_map/all_gather | solution.py:18
  7.3 140.9 %reduce-scatter.2.cloned.1.call-start = ((), (), s32[]{:S(2)}) async-start(), calls=%async_computation.3 | async-start | bytes 2359296 | tf_op jit(solution)/shard_map/reduce_scatter | solution.py:23
  106.0 42.2 %copy-start.2 = (bf16[1024,64]{0,1:T(8,128)(2,1)S(1)}, bf16[1024,64]{0,1:T(8,128)(2,1)}, u32[]{:S(2)}) copy-start(bf16[1024,64]{0,1:T(8,128)(2,1)} %param.9) | copy-start | bytes 393220
  148.2 33.3 %copy-start.3 = (f32[1024,64]{0,1:T(8,128)S(1)}, f32[1024,64]{0,1:T(8,128)}, u32[]{:S(2)}) copy-start(f32[1024,64]{0,1:T(8,128)} %reduce-scatter.2.cloned.1.call-done) | copy-start | bytes 786436
  181.5 3.7 %copy-start = (bf16[2048,1024]{1,0:T(8,128)(2,1)S(1)}, bf16[2048,1024]{1,0:T(8,128)(2,1)}, u32[]{:S(2)}) copy-start(bf16[2048,1024]{1,0:T(8,128)(2,1)} %param.8) | copy-start | bytes 12582916
  216.1 3.7 %copy-start.1 = (bf16[2048,1024]{1,0:T(8,128)(2,1)S(1)}, bf16[2048,1024]{1,0:T(8,128)(2,1)}, u32[]{:S(2)}) copy-start(bf16[2048,1024]{1,0:T(8,128)(2,1)} %param.8) | copy-start | bytes 12582916
Sparse Core Ops, SparseCore 0:
  8.9 39.7 all-gather.1
  107.7 40.4 reduce-scatter.1
where the time goes:
time: 293 us
  blocking collectives  167 us (57%)
  waiting for transfers between devices  82.7 us (28%)
  matrix products  27 us (9%)
  between operations  13.5 us (5%)
    psum x4, blocking collectives, body(): newest = lax.psum(term, 'blk').astype(jnp.bfloat16)  117 us
    all_to_all x1, blocking collectives, body(): lax.all_to_all(partial_value, 'slab', split_axis=1, concat_axis=0, tiled=...  50.4 us
    all_gather x1, waiting for transfers between devices, body(): lax.all_gather(solved, 'slab', axis=1, tiled=True)  41.4 us
    reduce_scatter x1, waiting for transfers between devices, body(): lax.psum_scatter(window_terms, 'blk', scatter_dimension=0, tiled=True)  40.6 us
    dot_general x4, matrix products, body(): term = jnp.dot(inv_diag, resid, preferred_element_type=jnp.float32)  12.6 us
    dot_general x2, matrix products, body(): update = jnp.dot(columns, newest, preferred_element_type=jnp.float32)  7.47 us
    dot_general x1, matrix products, body(): jnp.dot(old_factor, lax.all_gather(solved, 'slab', axis=1, tiled=True), p...  6.89 us
  transfers between devices with their start and end apart: 2, of which 2 were waited for; matrix products, arithmetic and copies ran while one was open for 0% of the time, Pallas kernels for 0%

commit v1 on v0

--- a/solution.py
+++ b/solution.py
@@ -4,6 +4,28 @@
 from jax.sharding import PartitionSpec as P
 
 STEPS = 4
+
+
+def joined_along(blocks, dim):
+    blocks = jnp.moveaxis(blocks, 0, dim)
+    shape = blocks.shape
+    return blocks.reshape(*shape[:dim], shape[dim] * shape[dim + 1], *shape[dim + 2 :])
+
+
+def ring_gather(shard, axis, dim):
+    size = lax.axis_size(axis)
+    pairs = [(i, (i + 1) % size) for i in range(size)]
+    back = [(b, a) for a, b in pairs]
+    lower, upper = ([], [])
+    for step in range(size - 1):
+        if step % 2 == 0:
+            lower.append(lax.ppermute(lower[-1] if lower else shard, axis, pairs))
+        else:
+            upper.append(lax.ppermute(upper[-1] if upper else shard, axis, back))
+    tiles = jnp.stack([*lower[::-1], shard, *upper])
+    shift = lax.axis_index(axis) - len(lower)
+    tiles = tiles[(jnp.arange(size) - shift) % size]
+    return joined_along(tiles, dim)
 
 
 def body(old_factor, solved, band, inv_diag, rhs):
@@ -14,9 +36,7 @@
     own_block = own_index // group_size
     offset = own_index % group_size * own_rows
     partial_value = jnp.dot(
-        old_factor,
-        lax.all_gather(solved, "slab", axis=1, tiled=True),
-        preferred_element_type=jnp.float32,
+        old_factor, ring_gather(solved, "slab", 1), preferred_element_type=jnp.float32
     )
     window_terms = lax.all_to_all(partial_value, "slab", split_axis=1, concat_axis=0, tiled=True)
     source = rhs.astype(jnp.float32)

time: 293 us -> 281 us (0.959)
  waiting for transfers between devices: 82.7 us -> 66.5 us
  starting transfers between devices: 0.04 us -> 5.08 us
    all_gather x1 -> x0, waiting for transfers between devices: 41.4 us -> none  [body(): lax.all_gather(solved, 'slab', axis=1, tiled=True)]
    ppermute x0 -> x3, waiting for transfers between devices: none -> 26.2 us  [the longest x2 19 us: ring_gather(): lower.append(lax.ppermute(lower[-1] if lower else shard, axis, pairs))]
    ppermute x0 -> x3, starting transfers between devices: none -> 5.08 us  [the longest x2 3.05 us: ring_gather(): lower.append(lax.ppermute(lower[-1] if lower else shard, axis, pairs))]
  transfers between devices with their start and end apart: 2 -> 4, of which waited for: 2 -> 4; matrix products, arithmetic and copies ran while one was open for 0% -> 0% of each run, Pallas kernels for 0% -> 0%
where the time goes in v1:
time: 281 us
  blocking collectives  165 us (59%)
  waiting for transfers between devices  66.5 us (24%)
  matrix products  26.6 us (9%)
  between operations  13.5 us (5%)
  starting transfers between devices  5.08 us (2%)
    psum x4, blocking collectives, body(): newest = lax.psum(term, 'blk').astype(jnp.bfloat16)  116 us
    all_to_all x1, blocking collectives, body(): lax.all_to_all(partial_value, 'slab', split_axis=1, concat_axis=0, tiled=...  48.7 us
    reduce_scatter x1, waiting for transfers between devices, body(): lax.psum_scatter(window_terms, 'blk', scatter_dimension=0, tiled=True)  40.3 us
    ppermute x2, waiting for transfers between devices, ring_gather(): lower.append(lax.ppermute(lower[-1] if lower else shard, axis, pairs))  19 us
    dot_general x4, matrix products, body(): term = jnp.dot(inv_diag, resid, preferred_element_type=jnp.float32)  12.6 us
    dot_general x2, matrix products, body(): update = jnp.dot(columns, newest, preferred_element_type=jnp.float32)  7.47 us
    ppermute x1, waiting for transfers between devices, ring_gather(): upper.append(lax.ppermute(upper[-1] if upper else shard, axis, back))  7.18 us
    dot_general x1, matrix products, body(): jnp.dot(old_factor, ring_gather(solved, 'slab', 1), preferred_element_typ...  6.47 us
  transfers between devices with their start and end apart: 4, of which 4 were waited for; matrix products, arithmetic and copies ran while one was open for 0% of the time, Pallas kernels for 0%

profile of v1, /device:TPU:0, one launch (start us, length us, event | category | flops | bytes accessed | tf_op | source)
XLA Modules:
  0.0 281.0 jit_solution(1706611519335076434)
XLA Ops:
  6.5 0.0 reduce-scatter.2.cloned.1.call-start
  6.5 3.1 %collective-permute-start = (bf16[3072,64]{0,1:T(8,128)(2,1)}, bf16[3072,64]{0,1:T(8,128)(2,1)S(1)}, u32[]{:S(2)}, u32[]{:S(2)}) collective-permute-start(bf16[3072,64]{0,1:T(8,128)(2,1)} %param.6), channel_id=1, source_target_pairs={{0,1},{1,2},{2,3},{3,0},{4,5},{5,6},{6,7},{7,4},{8,9},{9,10},{10,1... | collective-permute-start | bytes 1179656 | tf_op jit(solution)/shard_map/ppermute | solution.py:22
  9.6 2.0 collective-permute-start.2
  11.6 10.2 %collective-permute-done = bf16[3072,64]{0,1:T(8,128)(2,1)S(1)} collective-permute-done((bf16[3072,64]{0,1:T(8,128)(2,1)}, bf16[3072,64]{0,1:T(8,128)(2,1)S(1)}, u32[]{:S(2)}, u32[]{:S(2)}) %collective-permute-start) | collective-permute-done | bytes 393248 | tf_op jit(solution)/shard_map/ppermute | solution.py:22
  21.8 0.0 collective-permute-start.1
  21.9 7.2 %collective-permute-done.2 = bf16[3072,64]{0,1:T(8,128)(2,1)S(1)} collective-permute-done((bf16[3072,64]{0,1:T(8,128)(2,1)}, bf16[3072,64]{0,1:T(8,128)(2,1)S(1)}, u32[]{:S(2)}, u32[]{:S(2)}) %collective-permute-start.2) | collective-permute-done | bytes 393248 | tf_op jit(solution)/shard_map/ppermute | solution.py:24
  29.0 8.8 %collective-permute-done.1 = bf16[3072,64]{0,1:T(8,128)(2,1)S(1)} collective-permute-done((bf16[3072,64]{0,1:T(8,128)(2,1)S(1)}, bf16[3072,64]{0,1:T(8,128)(2,1)S(1)}, u32[]{:S(2)}, u32[]{:S(2)}) %collective-permute-start.1) | collective-permute-done | bytes 393248 | tf_op jit(solution)/shard_map/ppermute | solution.py:22
  37.8 1.2 pad_maximum_fusion
  39.0 0.6 gather_fusion
  39.7 6.5 %fusion.58 = f32[256,2048]{1,0:T(8,128)S(1)} fusion(bf16[3072,256]{0,1:T(8,128)(2,1)S(1)} %bitcast.52, bf16[2048,3072]{1,0:T(8,128)(2,1)} %param.5), kind=kOutput, calls=%fused_computation.46 | convolution fusion | flops 3221225472 | bytes 16252928 | tf_op jit(solution)/shard_map/dot_general | solution.py:38
  46.2 48.7 %all_to_all.19 = f32[2048,4,64]{0,2,1:T(8,128)S(1)} all-to-all(f32[2048,4,64]{0,2,1:T(8,128)S(1)} %bitcast.53), channel_id=1, replica_groups=mesh['blk'=8,'slab'=4] {'slab'}, dimensions={1} | all-to-all | bytes 4194304 | tf_op jit(solution)/shard_map/all_to_all | solution.py:41
  94.9 0.0 copy-start.2
  94.9 1.5 copy.7
  96.4 0.0 reduce-scatter.2.cloned.1.call-update
  96.4 40.3 %reduce-scatter.2.cloned.1.call-done = f32[1024,64]{0,1:T(8,128)} async-done(((f32[8192,64]{0,1:T(8,128)}), f32[1024,64]{0,1:T(8,128)}) %reduce-scatter.2.cloned.1.call-update) | async-done | bytes 262160 | tf_op jit(solution)/shard_map/reduce_scatter | solution.py:43
  136.7 0.0 copy-done.2
  136.7 3.7 %fusion.6 = f32[2048,64]{0,1:T(8,128)S(1)} fusion(bf16[2048,1024]{1,0:T(8,128)(2,1)} %param.8, pred[]{:T(512)S(6)} %eq.21, f32[1024,64]{0,1:T(8,128)} %reduce-scatter.2.cloned.1.call-done, bf16[1024,64]{0,1:T(8,128)(2,1)S(1)} %copy-done.2), kind=kOutput, calls=%fused_computation.11 | convolution fusion | flops 268763136 | bytes 5111809 | tf_op jit(solution)/shard_map/dot_general | solution.py:48
  140.4 29.6 %all-reduce.4 = bf16[2048,64]{0,1:T(8,128)(2,1)S(1)} all-reduce(f32[2048,64]{0,1:T(8,128)S(1)} %fusion.6), channel_id=1, replica_groups=mesh['blk'=8,'slab'=4] {'blk'}, use_global_device_ids=true, to_apply=%region_1.2 | all-reduce | flops 131072 | bytes 786432 | tf_op jit(solution)/shard_map/psum | solution.py:50
  170.1 0.0 copy-done.3
  170.1 0.0 copy-start
  170.1 3.7 %fusion.16 = f32[1024,64]{0,1:T(8,128)S(1)} fusion(f32[1024,64]{0,1:T(8,128)S(1)} %copy-done.3, bf16[2048,64]{0,1:T(8,128)(2,1)S(1)} %all-reduce.4, bf16[1024,8192]{1,0:T(8,128)(2,1)} %param.7, pred[]{:T(512)S(6)} %gt.9), kind=kOutput, calls=%fused_computation.18 | convolution fusion | flops 268566528 | bytes 4980737 | tf_op jit(solution)/shard_map/dot_general | solution.py:55
  173.9 0.0 copy-done
  173.9 1.4 fusion.7
  175.3 29.2 %all-reduce.5 = bf16[2048,64]{0,1:T(8,128)(2,1)S(1)} all-reduce(f32[2048,64]{0,1:T(8,128)S(1)} %fusion.7), channel_id=1, replica_groups=mesh['blk'=8,'slab'=4] {'blk'}, use_global_device_ids=true, to_apply=%region_2.3 | all-reduce | flops 131072 | bytes 786432 | tf_op jit(solution)/shard_map/psum | solution.py:50
  204.5 0.0 copy-start.1
  204.5 3.7 %fusion.25 = f32[1024,64]{0,1:T(8,128)S(1)} fusion(f32[1024,64]{0,1:T(8,128)S(1)} %fusion.16, bf16[2048,64]{0,1:T(8,128)(2,1)S(1)} %all-reduce.5, bf16[1024,8192]{1,0:T(8,128)(2,1)} %param.7, pred[]{:T(512)S(6)} %gt.10), kind=kOutput, calls=%fused_computation.21 | convolution fusion | flops 268566528 | bytes 4980737 | tf_op jit(solution)/shard_map/dot_general | solution.py:55
  208.3 0.0 copy-done.1
  208.3 1.4 fusion.8
  209.7 28.8 %all-reduce.6 = bf16[2048,64]{0,1:T(8,128)(2,1)S(1)} all-reduce(f32[2048,64]{0,1:T(8,128)S(1)} %fusion.8), channel_id=1, replica_groups=mesh['blk'=8,'slab'=4] {'blk'}, use_global_device_ids=true, to_apply=%region_3.4 | all-reduce | flops 131072 | bytes 786432 | tf_op jit(solution)/shard_map/psum | solution.py:50
  238.4 6.2 %fusion.9 = f32[2048,64]{0,1:T(8,128)S(1)} fusion(bf16[2048,1024]{1,0:T(8,128)(2,1)} %param.8, f32[1024,64]{0,1:T(8,128)S(1)} %fusion.25, bf16[2048,64]{0,1:T(8,128)(2,1)S(1)} %all-reduce.6, bf16[1024,8192]{1,0:T(8,128)(2,1)} %param.7, bf16[1024,64]{0,1:T(8,128)(2,1)S(1)} %copy-done.2, pred[]{:T(512)S(6)} %eq.20, pred[]{:T(512)S(6)} %gt.11), kind=kOutput, calls=%fused_computation.14 | convolution fusion | flops 537329664 | bytes 9568258 | tf_op jit(solution)/shard_map/dot_general | solution.py:48
  244.6 28.8 %all-reduce.7 = bf16[2048,64]{0,1:T(8,128)(2,1)S(1)} all-reduce(f32[2048,64]{0,1:T(8,128)S(1)} %fusion.9), channel_id=1, replica_groups=mesh['blk'=8,'slab'=4] {'blk'}, use_global_device_ids=true, to_apply=%region_4.5 | all-reduce | flops 131072 | bytes 786432 | tf_op jit(solution)/shard_map/psum | solution.py:50
  273.4 0.7 fusion.49
  (3 shorter events, 0.0 us)
Async XLA Ops:
  6.5 130.2 %reduce-scatter.2.cloned.1.call-start = ((), (), s32[]{:S(2)}) async-start(), calls=%async_computation.2 | async-start | bytes 2359296 | tf_op jit(solution)/shard_map/reduce_scatter | solution.py:43
  6.5 15.3 %collective-permute-start = (bf16[3072,64]{0,1:T(8,128)(2,1)}, bf16[3072,64]{0,1:T(8,128)(2,1)S(1)}, u32[]{:S(2)}, u32[]{:S(2)}) collective-permute-start(bf16[3072,64]{0,1:T(8,128)(2,1)} %param.6), channel_id=1, source_target_pairs={{0,1},{1,2},{2,3},{3,0},{4,5},{5,6},{6,7},{7,4},{8,9},{9,10},{10,1... | collective-permute-start | bytes 1179656 | tf_op jit(solution)/shard_map/ppermute | solution.py:22
  9.6 19.5 %collective-permute-start.2 = (bf16[3072,64]{0,1:T(8,128)(2,1)}, bf16[3072,64]{0,1:T(8,128)(2,1)S(1)}, u32[]{:S(2)}, u32[]{:S(2)}) collective-permute-start(bf16[3072,64]{0,1:T(8,128)(2,1)} %param.6), channel_id=1, source_target_pairs={{1,0},{2,1},{3,2},{0,3},{5,4},{6,5},{7,6},{4,7},{9,8},{10,9},{11,1... | collective-permute-start | bytes 1179656 | tf_op jit(solution)/shard_map/ppermute | solution.py:24
  21.8 16.0 %collective-permute-start.1 = (bf16[3072,64]{0,1:T(8,128)(2,1)S(1)}, bf16[3072,64]{0,1:T(8,128)(2,1)S(1)}, u32[]{:S(2)}, u32[]{:S(2)}) collective-permute-start(bf16[3072,64]{0,1:T(8,128)(2,1)S(1)} %collective-permute-done), channel_id=1, source_target_pairs={{0,1},{1,2},{2,3},{3,0},{4,5},{5,6},{6,7},{7,4},{8,9},{9,10},{10,1... | collective-permute-start | bytes 1179656 | tf_op jit(solution)/shard_map/ppermute | solution.py:22
  94.9 41.9 %copy-start.2 = (bf16[1024,64]{0,1:T(8,128)(2,1)S(1)}, bf16[1024,64]{0,1:T(8,128)(2,1)}, u32[]{:S(2)}) copy-start(bf16[1024,64]{0,1:T(8,128)(2,1)} %param.9) | copy-start | bytes 393220
  136.7 33.4 %copy-start.3 = (f32[1024,64]{0,1:T(8,128)S(1)}, f32[1024,64]{0,1:T(8,128)}, u32[]{:S(2)}) copy-start(f32[1024,64]{0,1:T(8,128)} %reduce-scatter.2.cloned.1.call-done) | copy-start | bytes 786436
  170.1 3.8 %copy-start = (bf16[2048,1024]{1,0:T(8,128)(2,1)S(1)}, bf16[2048,1024]{1,0:T(8,128)(2,1)}, u32[]{:S(2)}) copy-start(bf16[2048,1024]{1,0:T(8,128)(2,1)} %param.8) | copy-start | bytes 12582916
  204.5 3.8 %copy-start.1 = (bf16[2048,1024]{1,0:T(8,128)(2,1)S(1)}, bf16[2048,1024]{1,0:T(8,128)(2,1)}, u32[]{:S(2)}) copy-start(bf16[2048,1024]{1,0:T(8,128)(2,1)} %param.8) | copy-start | bytes 12582916
Sparse Core Ops, SparseCore 0:
  96.5 40.1 reduce-scatter.1
